TPU v7x, 128 devices: a whole 4x4x4 slice. The times are simulated.
128 devices in a mesh: member: 16 (over z, x_lo, core), tensor: 8 (over y, x_hi).
Axes of the slice: x: 4 (x_hi: 2, x_lo: 2; x = x_hi * 2 + x_lo), y: 4, z: 4, core: 2. Of those that a mesh axis runs over, the one named last changes fastest.
Arguments:
- query: bfloat16 [8192, 8192], P('member', 'tensor'), may hold values from -100 to 100
- keys: bfloat16 [8192, 1024], P('member', 'tensor'), may hold values from -6 to 6
- values: bfloat16 [8192, 1024], P('member', 'tensor'), may hold values from -12 to 12
- residual: bfloat16 [8192, 8192], P('member', 'tensor'), may hold values from -6 to 6
- out_weight: bfloat16 [8192, 8192], P('tensor', 'member'), may hold values from -0.0625 to 0.0625
- norm_gain: float32 [8192], replicated, may hold values from 0.1 to 1.9
- cand_len: int32 [64], P('member'), may hold values from 32 to 128, as said below
- head_w1: bfloat16 [16, 8192, 4096], P('member', None, 'tensor'), may hold values from -0.0625 to 0.0625
- head_b1: float32 [16, 4096], P('member', 'tensor'), may hold values from -3 to 3
- head_w2: bfloat16 [16, 4096, 4096], P('member', 'tensor'), may hold values from -0.09375 to 0.09375
- head_b2: float32 [16, 4096], P('member'), may hold values from -3 to 3
- head_w3: bfloat16 [16, 4096], P('member'), may hold values from -0.09375 to 0.09375
- head_b3: float32 [16], P('member'), may hold values from -4 to 4
Outputs:
- trunk_out: bfloat16 [8192, 8192], P('member', 'tensor')
- scores: float32 [16, 64], P('member')
Inputs may be any that keep to these rules, and one draw needn't show every extreme that they name: Token slots of candidate c at places cand_len[c] and beyond are padding: excluded as keys, and the slot at place cand_len[c] - 1 is the one that is scored.
All inputs are finite; a program needn't handle non-finite values.
Results may differ from a plain program's by a relative error of at most 0.014.
Values may be sent and summed in bfloat16 or wider, within the bound.
No kernel may reach another device: no remote copies, remote signals or barrier semaphores. Data moves between devices by JAX's collectives and lax.ppermute only.
A program may use at most 192 MiB of HBM per device.

v0:
```python
import jax
import jax.numpy as jnp
from jax import lax
from jax.sharding import PartitionSpec as P

HEAD_WIDTH = 128
SEQUENCE_SLOTS = 128


def local(
    query,
    keys,
    values,
    residual,
    out_weight,
    norm_gain,
    cand_len,
    head_w1,
    head_b1,
    head_w2,
    head_b2,
    head_w3,
    head_b3,
):
    row_count = query.shape[0]
    cand_count = row_count // SEQUENCE_SLOTS
    heads_here = query.shape[1] // HEAD_WIDTH
    kv_here = keys.shape[1] // HEAD_WIDTH
    group_width = heads_here // kv_here
    query_tiles = query.reshape(cand_count, SEQUENCE_SLOTS, kv_here, group_width, HEAD_WIDTH)
    key_tiles = keys.reshape(cand_count, SEQUENCE_SLOTS, kv_here, HEAD_WIDTH)
    value_tiles = values.reshape(cand_count, SEQUENCE_SLOTS, kv_here, HEAD_WIDTH)
    logits = jnp.einsum(
        "cskgd,ctkd->ckgst", query_tiles, key_tiles, preferred_element_type=jnp.float32
    ) * HEAD_WIDTH ** (-0.5)
    places = jnp.arange(SEQUENCE_SLOTS, dtype=jnp.int32)
    allowed = (places[None, :, None] >= places[None, None, :]) & (
        places[None, None, :] < cand_len[:, None, None]
    )
    allowed = allowed[:, None, None]
    logits = jnp.where(allowed, logits, jnp.float32(-1e30))
    row_max = jnp.max(logits, axis=-1, keepdims=True)
    probs = jnp.where(allowed, jnp.exp(logits - row_max), jnp.float32(0.0))
    totals = jnp.sum(probs, axis=-1, keepdims=True)
    attn_weights = (probs / totals).astype(jnp.bfloat16)
    attn_out = jnp.einsum(
        "ckgst,ctkd->cskgd", attn_weights, value_tiles, preferred_element_type=jnp.float32
    )
    attn_out = attn_out.astype(jnp.bfloat16).reshape(row_count, heads_here * HEAD_WIDTH)
    projected = jnp.dot(
        attn_out,
        lax.all_gather(out_weight, "member", axis=1, tiled=True),
        preferred_element_type=jnp.float32,
    )
    summed = lax.psum_scatter(
        projected.astype(jnp.bfloat16), "tensor", scatter_dimension=1, tiled=True
    ).astype(jnp.float32)
    trunk_out = (summed + residual.astype(jnp.float32)).astype(jnp.bfloat16)
    last_rows = jnp.arange(cand_count, dtype=jnp.int32) * SEQUENCE_SLOTS + cand_len - 1
    picked = jnp.take(trunk_out, last_rows, axis=0)
    full_rows = lax.all_gather(picked, "tensor", axis=1, tiled=True).astype(jnp.float32)
    mean_square = jnp.mean(full_rows * full_rows, axis=-1, keepdims=True) + 1e-05
    features = (full_rows * lax.rsqrt(mean_square) * norm_gain).astype(jnp.bfloat16)
    all_features = lax.all_gather(features, "member", axis=0, tiled=True)
    first = jax.nn.silu(
        jnp.dot(all_features, head_w1[0], preferred_element_type=jnp.float32) + head_b1[0]
    ).astype(jnp.bfloat16)
    hidden_terms = jnp.dot(first, head_w2[0], preferred_element_type=jnp.float32)
    second = jax.nn.silu(
        lax.psum(hidden_terms.astype(jnp.bfloat16), "tensor").astype(jnp.float32) + head_b2[0]
    )
    scores = jnp.sum(second * head_w3[0].astype(jnp.float32), axis=-1) + head_b3[0]
    return (trunk_out, scores[None, :])


def solution(mesh):
    in_specs = (
        P("member", "tensor"),
        P("member", "tensor"),
        P("member", "tensor"),
        P("member", "tensor"),
        P("tensor", "member"),
        P(),
        P("member"),
        P("member", None, "tensor"),
        P("member", "tensor"),
        P("member", "tensor", None),
        P("member", None),
        P("member", None),
        P("member"),
    )
    out_specs = (P("member", "tensor"), P("member", None))
    return jax.shard_map(local, mesh=mesh, in_specs=in_specs, out_specs=out_specs, check_vma=False)
```

profile of v0, /device:TPU:0, one launch (start us, length us, event | category | flops | bytes accessed | tf_op | source)
XLA Modules:
  0.0 407.6 jit_solution(14648535822901284644)
XLA Ops:
  7.2 0.0 copy-start
  7.2 0.0 all-gather.4.cloned.1.call-start
  7.2 0.7 all-gather.4.cloned.1.call-update
  7.9 0.0 reduce-scatter.2.cloned.1.call-start
  8.0 1.5 copy.26
  9.5 0.1 iota_compare_fusion.1
  9.6 0.1 broadcast_and_fusion
  9.7 0.5 fusion.3
  10.2 0.6 fusion.4
  10.8 0.9 fusion.5
  11.7 0.7 copy.22
  12.4 91.4 %all-gather.4.cloned.1.call-done = bf16[1024,8192]{1,0:T(8,128)(2,1)} async-done(((bf16[1024,512]{1,0:T(8,128)(2,1)}), bf16[1024,8192]{1,0:T(8,128)(2,1)}) %all-gather.4.cloned.1.call-update) | async-done | bytes 16777232 | tf_op jit(solution)/shard_map/all_gather | solution.py:52
  103.8 16.8 %convolution_convert_fusion = bf16[512,8192]{1,0:T(8,128)(2,1)} fusion(bf16[1024,8192]{1,0:T(8,128)(2,1)} %all-gather.4.cloned.1.call-done, bf16[64,8,8,128]{3,2,1,0:T(8,128)(2,1)S(1)} %bitcast.71), kind=kOutput, calls=%fused_computation.1 | convolution fusion | flops 8594128896 | bytes 26214400 | tf_op jit(solution)/shard_map/dot_general | solution.py:50
  120.6 0.0 reduce-scatter.2.cloned.1.call-update
  120.6 0.0 all-gather.6.cloned.1.call-start
  120.7 115.5 %reduce-scatter.2.cloned.1.call-done = bf16[512,1024]{1,0:T(8,128)(2,1)} async-done(((bf16[512,8192]{1,0:T(8,128)(2,1)}), bf16[512,1024]{1,0:T(8,128)(2,1)}) %reduce-scatter.2.cloned.1.call-update) | async-done | bytes 1048592 | tf_op jit(solution)/shard_map/reduce_scatter | solution.py:55
  236.2 1.6 add_convert_fusion
  237.8 0.0 copy-start.1
  237.8 0.6 gather_fusion
  238.4 0.1 broadcast_select_fusion
  238.5 34.2 %all_gather.10 = bf16[4,8192]{1,0:T(4,128)(2,1)S(1)} all-gather(bf16[4,1024]{1,0:T(4,128)(2,1)S(1)} %broadcast_select_fusion), channel_id=1, replica_groups=mesh['member'=16,'tensor'=8] {'tensor'}, dimensions={1}, use_global_device_ids=true | all-gather | bytes 73728 | tf_op jit(solution)/shard_map/all_gather | solution.py:61
  272.7 0.2 fusion.15
  272.9 0.7 fusion.22
  273.6 0.0 all-gather.6.cloned.1.call-update
  273.7 0.0 all-reduce.2.cloned.1.call-start
  273.7 30.1 %all-gather.6.cloned.1.call-done = bf16[16,4,8192]{2,1,0:T(4,128)(2,1)} async-done(((bf16[1,4,8192]{2,1,0:T(4,128)(2,1)}), bf16[16,4,8192]{2,1,0:T(4,128)(2,1)}) %all-gather.6.cloned.1.call-update) | async-done | bytes 1048592 | tf_op jit(solution)/shard_map/all_gather | solution.py:64
  303.8 1.3 reshape.118
  305.2 7.8 %convolution_convert_fusion.1 = bf16[64,4096]{1,0:T(8,128)(2,1)} fusion(bf16[1,512,4096]{2,1,0:T(8,128)(2,1)} %param.22, bf16[64,8192]{1,0:T(8,128)(2,1)S(1)} %reshape.118, bf16[1,8192,512]{2,1,0:T(8,128)(2,1)} %param.20, f32[512]{0:T(512)S(1)} %bitcast.74), kind=kOutput, calls=%fused_computation.4 | convolution fusion | flops 805765120 | bytes 14157824 | tf_op jit(solution)/shard_map/dot_general | solution.py:68
  312.9 0.0 all-reduce.2.cloned.1.call-update
  313.6 85.4 %all-reduce.2.cloned.1.call-done = bf16[64,4096]{1,0:T(8,128)(2,1)} async-done(((bf16[64,4096]{1,0:T(8,128)(2,1)}), bf16[64,4096]{1,0:T(8,128)(2,1)}) %all-reduce.2.cloned.1.call-update) | async-done | bytes 524304 | tf_op jit(solution)/shard_map/psum | solution.py:70
  399.1 1.5 multiply_reduce_fusion
  400.5 0.5 add_bitcast_fusion
  (21 shorter events, 0.1 us)
Async XLA Ops:
  7.2 2.6 copy-start
  7.2 2.3 copy-start.8
  7.2 96.6 %all-gather.4.cloned.1.call-start = ((), (), s32[]{:S(2)}) async-start(), calls=%async_computation.1 | async-start | bytes 17825792 | tf_op jit(solution)/shard_map/all_gather | solution.py:52
  7.9 228.3 %reduce-scatter.2.cloned.1.call-start = ((), (), s32[]{:S(2)}) async-start(), calls=%async_computation.2 | async-start | bytes 9437184 | tf_op jit(solution)/shard_map/reduce_scatter | solution.py:55
  9.7 1.1 copy-start.7
  120.6 115.6 %copy-start.2 = (bf16[512,1024]{1,0:T(8,128)(2,1)S(1)}, bf16[512,1024]{1,0:T(8,128)(2,1)}, u32[]{:S(2)}) copy-start(bf16[512,1024]{1,0:T(8,128)(2,1)} %param.16) | copy-start | bytes 3145732
  120.6 152.3 %copy-start.3 = (f32[8192]{0:T(1024)S(1)}, f32[8192]{0:T(1024)}, u32[]{:S(2)}) copy-start(f32[8192]{0:T(1024)} %param.18) | copy-start | bytes 98308
  120.6 183.2 %all-gather.6.cloned.1.call-start = ((), (), s32[]{:S(2)}) async-start(), calls=%async_computation.4 | async-start | bytes 1114112 | tf_op jit(solution)/shard_map/all_gather | solution.py:64
  120.7 184.4 %copy-start.6 = (f32[1,512]{1,0:T(1,128)S(1)}, f32[1,512]{1,0:T(1,128)}, u32[]{:S(2)}) copy-start(f32[1,512]{1,0:T(1,128)} %param.21) | copy-start | bytes 6148
  237.8 75.1 %copy-start.1 = (bf16[512,1024]{1,0:T(8,128)(2,1)}, bf16[512,1024]{1,0:T(8,128)(2,1)S(1)}, u32[]{:S(2)}) copy-start(bf16[512,1024]{1,0:T(8,128)(2,1)S(1)} %add_convert_fusion) | copy-start | bytes 3145732
  273.7 125.4 %all-reduce.2.cloned.1.call-start = ((), (), s32[]{:S(2)}) async-start(), calls=%async_computation.3 | async-start | bytes 1048576 | tf_op jit(solution)/shard_map/psum | solution.py:70
  305.2 7.8 %copy-start.5 = (bf16[1,4096]{1,0:T(2,128)(2,1)S(1)}, bf16[1,4096]{1,0:T(2,128)(2,1)}, u32[]{:S(2)}) copy-start(bf16[1,4096]{1,0:T(2,128)(2,1)} %param.24) | copy-start | bytes 24580
  305.2 93.9 %copy-start.4 = (f32[1,4096]{1,0:T(1,128)S(1)}, f32[1,4096]{1,0:T(1,128)}, u32[]{:S(2)}) copy-start(f32[1,4096]{1,0:T(1,128)} %param.23) | copy-start | bytes 49156
Sparse Core Ops, SparseCore 0:
  9.7 94.0 all-gather.3
  120.8 115.3 reduce-scatter.1
  273.8 29.9 all-gather.5
  313.1 85.9 all-reduce.1
where the time goes:
time: 408 us
  waiting for transfers between devices  323 us (79%)
  blocking collectives  34.2 us (8%)
  matrix products  25.9 us (6%)
  between operations  14.6 us (4%)
  other arithmetic  5.43 us (1%)
  local copies, waits for them, and re-layouts  4.13 us (1%)
    reduce_scatter x1, waiting for transfers between devices, local(): lax.psum_scatter(projected.astype(jnp.bfloat16), 'tensor', scatter_dimens...  115 us
    all_gather x1, waiting for transfers between devices, local(): lax.all_gather(out_weight, 'member', axis=1, tiled=True)  91.4 us
    psum x1, waiting for transfers between devices, local(): lax.psum(hidden_terms.astype(jnp.bfloat16), 'tensor').astype(jnp.float32)  85.4 us
    all_gather x1, blocking collectives, local(): lax.all_gather(picked, 'tensor', axis=1, tiled=True).astype(jnp.float32)  34.2 us
    all_gather x1, waiting for transfers between devices, local(): all_features = lax.all_gather(features, 'member', axis=0, tiled=True)  30.1 us
    dot_general x1, matrix products, local(): jnp.dot(attn_out, lax.all_gather(out_weight, 'member', axis=1, tiled=True...  16.8 us
  transfers between devices with their start and end apart: 4, of which 4 were waited for; matrix products, arithmetic and copies ran while one was open for 1% of the time, Pallas kernels for 0%

commit v1 on v0

--- a/solution.py
+++ b/solution.py
@@ -67,7 +67,10 @@
     ).astype(jnp.bfloat16)
     hidden_terms = jnp.dot(first, head_w2[0], preferred_element_type=jnp.float32)
     second = jax.nn.silu(
-        lax.psum(hidden_terms.astype(jnp.bfloat16), "tensor").astype(jnp.float32) + head_b2[0]
+        jnp.sum(lax.all_gather(hidden_terms.astype(jnp.bfloat16), "tensor"), axis=0).astype(
+            jnp.float32
+        )
+        + head_b2[0]
     )
     scores = jnp.sum(second * head_w3[0].astype(jnp.float32), axis=-1) + head_b3[0]
     return (trunk_out, scores[None, :])

time: 408 us -> 395 us (0.968)
  waiting for transfers between devices: 323 us -> 308 us
    psum x1 -> x0, waiting for transfers between devices: 85.4 us -> none  [local(): lax.psum(hidden_terms.astype(jnp.bfloat16), 'tensor').astype(jnp.float32)]
    all_gather x0 -> x1, waiting for transfers between devices: none -> 70.7 us  [local(): lax.all_gather(hidden_terms.astype(jnp.bfloat16), 'tensor')]
where the time goes in v1:
time: 395 us
  waiting for transfers between devices  308 us (78%)
  blocking collectives  34.2 us (9%)
  matrix products  25.9 us (7%)
  between operations  14.6 us (4%)
  other arithmetic  7.34 us (2%)
  local copies, waits for them, and re-layouts  4.13 us (1%)
    reduce_scatter x1, waiting for transfers between devices, local(): lax.psum_scatter(projected.astype(jnp.bfloat16), 'tensor', scatter_dimens...  115 us
    all_gather x1, waiting for transfers between devices, local(): lax.all_gather(out_weight, 'member', axis=1, tiled=True)  91.4 us
    all_gather x1, waiting for transfers between devices, local(): lax.all_gather(hidden_terms.astype(jnp.bfloat16), 'tensor')  70.7 us
    all_gather x1, blocking collectives, local(): lax.all_gather(picked, 'tensor', axis=1, tiled=True).astype(jnp.float32)  34.2 us
    all_gather x1, waiting for transfers between devices, local(): all_features = lax.all_gather(features, 'member', axis=0, tiled=True)  30.1 us
    dot_general x1, matrix products, local(): jnp.dot(attn_out, lax.all_gather(out_weight, 'member', axis=1, tiled=True...  16.8 us
  transfers between devices with their start and end apart: 4, of which 4 were waited for; matrix products, arithmetic and copies ran while one was open for 1% of the time, Pallas kernels for 0%

profile of v1, /device:TPU:0, one launch (start us, length us, event | category | flops | bytes accessed | tf_op | source)
XLA Modules:
  0.0 394.8 jit_solution(752127735207965412)
XLA Ops:
  7.2 0.0 copy-start
  7.2 0.0 all-gather.6.cloned.1.call-start
  7.2 0.7 all-gather.6.cloned.1.call-update
  7.9 0.0 reduce-scatter.2.cloned.1.call-start
  8.0 1.5 copy.29
  9.5 0.1 iota_compare_fusion.1
  9.6 0.1 broadcast_and_fusion
  9.7 0.5 fusion.3
  10.2 0.6 fusion.4
  10.8 0.9 fusion.5
  11.7 0.7 copy.25
  12.4 91.4 %all-gather.6.cloned.1.call-done = bf16[1024,8192]{1,0:T(8,128)(2,1)} async-done(((bf16[1024,512]{1,0:T(8,128)(2,1)}), bf16[1024,8192]{1,0:T(8,128)(2,1)}) %all-gather.6.cloned.1.call-update) | async-done | bytes 16777232 | tf_op jit(solution)/shard_map/all_gather | solution.py:52
  103.8 16.8 %convolution_convert_fusion = bf16[512,8192]{1,0:T(8,128)(2,1)} fusion(bf16[1024,8192]{1,0:T(8,128)(2,1)} %all-gather.6.cloned.1.call-done, bf16[64,8,8,128]{3,2,1,0:T(8,128)(2,1)S(1)} %bitcast.73), kind=kOutput, calls=%fused_computation.1 | convolution fusion | flops 8594128896 | bytes 26214400 | tf_op jit(solution)/shard_map/dot_general | solution.py:50
  120.6 0.0 reduce-scatter.2.cloned.1.call-update
  120.6 0.0 all-gather.10.cloned.1.call-start
  120.7 115.5 %reduce-scatter.2.cloned.1.call-done = bf16[512,1024]{1,0:T(8,128)(2,1)} async-done(((bf16[512,8192]{1,0:T(8,128)(2,1)}), bf16[512,1024]{1,0:T(8,128)(2,1)}) %reduce-scatter.2.cloned.1.call-update) | async-done | bytes 1048592 | tf_op jit(solution)/shard_map/reduce_scatter | solution.py:55
  236.2 1.6 add_convert_fusion
  237.8 0.6 gather_fusion
  238.4 0.1 broadcast_select_fusion
  238.5 34.2 %all_gather.16 = bf16[4,8192]{1,0:T(4,128)(2,1)S(1)} all-gather(bf16[4,1024]{1,0:T(4,128)(2,1)S(1)} %broadcast_select_fusion), channel_id=1, replica_groups=mesh['member'=16,'tensor'=8] {'tensor'}, dimensions={1}, use_global_device_ids=true | all-gather | bytes 73728 | tf_op jit(solution)/shard_map/all_gather | solution.py:61
  272.7 0.2 fusion.15
  272.9 0.7 fusion.22
  273.6 0.0 all-gather.10.cloned.1.call-update
  273.7 0.0 all-gather.8.cloned.1.call-start
  273.7 30.1 %all-gather.10.cloned.1.call-done = bf16[16,4,8192]{2,1,0:T(4,128)(2,1)} async-done(((bf16[1,4,8192]{2,1,0:T(4,128)(2,1)}), bf16[16,4,8192]{2,1,0:T(4,128)(2,1)}) %all-gather.10.cloned.1.call-update) | async-done | bytes 1048592 | tf_op jit(solution)/shard_map/all_gather | solution.py:64
  303.8 1.3 reshape.119
  305.2 7.8 %convolution_convert_fusion.1 = bf16[64,4096]{1,0:T(8,128)(2,1)} fusion(bf16[1,512,4096]{2,1,0:T(8,128)(2,1)} %param.22, bf16[64,8192]{1,0:T(8,128)(2,1)S(1)} %reshape.119, bf16[1,8192,512]{2,1,0:T(8,128)(2,1)} %param.20, f32[512]{0:T(512)S(1)} %bitcast.76), kind=kOutput, calls=%fused_computation.4 | convolution fusion | flops 805765120 | bytes 14157824 | tf_op jit(solution)/shard_map/dot_general | solution.py:68
  312.9 0.0 all-gather.8.cloned.1.call-update
  313.7 70.7 %all-gather.8.cloned.1.call-done = bf16[512,4096]{1,0:T(8,128)(2,1)} async-done(((bf16[64,4096]{1,0:T(8,128)(2,1)}), bf16[512,4096]{1,0:T(8,128)(2,1)}) %all-gather.8.cloned.1.call-update) | async-done | bytes 4194320 | tf_op jit(solution)/shard_map/all_gather | solution.py:70
  384.4 3.0 reduce_sum.41
  387.4 0.4 multiply_reduce_fusion
  387.8 0.5 add_bitcast_fusion
  (22 shorter events, 0.1 us)
Async XLA Ops:
  7.2 2.6 copy-start
  7.2 2.3 copy-start.8
  7.2 96.6 %all-gather.6.cloned.1.call-start = ((), (), s32[]{:S(2)}) async-start(), calls=%async_computation.1 | async-start | bytes 17825792 | tf_op jit(solution)/shard_map/all_gather | solution.py:52
  7.9 228.3 %reduce-scatter.2.cloned.1.call-start = ((), (), s32[]{:S(2)}) async-start(), calls=%async_computation.2 | async-start | bytes 9437184 | tf_op jit(solution)/shard_map/reduce_scatter | solution.py:55
  9.7 1.1 copy-start.7
  120.6 115.6 %copy-start.2 = (bf16[512,1024]{1,0:T(8,128)(2,1)S(1)}, bf16[512,1024]{1,0:T(8,128)(2,1)}, u32[]{:S(2)}) copy-start(bf16[512,1024]{1,0:T(8,128)(2,1)} %param.16) | copy-start | bytes 3145732
  120.6 152.3 %copy-start.3 = (f32[8192]{0:T(1024)S(1)}, f32[8192]{0:T(1024)}, u32[]{:S(2)}) copy-start(f32[8192]{0:T(1024)} %param.18) | copy-start | bytes 98308
  120.6 183.2 %all-gather.10.cloned.1.call-start = ((), (), s32[]{:S(2)}) async-start(), calls=%async_computation.4 | async-start | bytes 1114112 | tf_op jit(solution)/shard_map/all_gather | solution.py:64
  120.7 184.4 %copy-start.6 = (f32[1,512]{1,0:T(1,128)S(1)}, f32[1,512]{1,0:T(1,128)}, u32[]{:S(2)}) copy-start(f32[1,512]{1,0:T(1,128)} %param.21) | copy-start | bytes 6148
  237.8 75.1 %copy-start.1 = (bf16[512,1024]{1,0:T(8,128)(2,1)}, bf16[512,1024]{1,0:T(8,128)(2,1)S(1)}, u32[]{:S(2)}) copy-start(bf16[512,1024]{1,0:T(8,128)(2,1)S(1)} %add_convert_fusion) | copy-start | bytes 3145732
  273.7 110.7 %all-gather.8.cloned.1.call-start = ((), (), s32[]{:S(2)}) async-start(), calls=%async_computation.3 | async-start | bytes 4718592 | tf_op jit(solution)/shard_map/all_gather | solution.py:70
  305.2 7.8 %copy-start.5 = (bf16[1,4096]{1,0:T(2,128)(2,1)S(1)}, bf16[1,4096]{1,0:T(2,128)(2,1)}, u32[]{:S(2)}) copy-start(bf16[1,4096]{1,0:T(2,128)(2,1)} %param.24) | copy-start | bytes 24580
  384.4 3.0 copy-start.4
Sparse Core Ops, SparseCore 0:
  9.7 94.0 all-gather.5
  120.8 115.3 reduce-scatter.1
  273.8 29.9 all-gather.9
  313.1 71.2 all-gather.7
